TPU v7x, 32 devices: a whole 2x2x4 slice. The times are simulated.
32 devices in a mesh: rows: 4 (over z), cols: 8 (over y, x, core).
Axes of the slice: x: 2, y: 2, z: 4, core: 2. Of those that a mesh axis runs over, the one named last changes fastest.
Arguments:
- genotypes: bfloat16 [30720, 2048], P(('rows', 'cols')), may hold values from 0 to 2
- probes: bfloat16 [30720, 128], P(('rows', 'cols')), may hold values from -6 to 6
- missing_codes: int32 [30720], P(('rows', 'cols')), may hold values from 0 to 31
Outputs:
- basis: bfloat16 [30720, 128], P(('rows', 'cols'))
- scores: bfloat16 [2048, 128], replicated
Inputs may be any that keep to these rules, and one draw needn't show every extreme that they name: `missing_codes`: A code c below 16 marks SNPs c * 128 to (c + 1) * 128 - 1 as missing for that individual; larger codes mark none.
All inputs are finite; a program needn't handle non-finite values.
Results may differ from a plain program's by a relative error of at most 0.017.
Values sent between devices are 32-bit elements; how exact they have to be, the bound alone decides.
A program may use at most 64 MiB of HBM per device.

v0:
```python
import math

import jax
import jax.numpy as jnp
from jax import lax
from jax.sharding import PartitionSpec as P

BLOCK_SNPS = 128


def everywhere(values):
    return lax.psum(values, ("rows", "cols"))


def statistics(moments):
    counted = jnp.maximum(moments[0], 1.0)
    mean = moments[1] / counted
    inv_sd = 1.0 / jnp.sqrt(moments[2] / counted - mean * mean + 1e-05)
    return (mean, inv_sd)


def per_device(genotypes, probes, missing_codes):
    snps = genotypes.shape[1]
    total_rows = genotypes.shape[0] * lax.axis_size("rows") * lax.axis_size("cols")
    blocks = snps // BLOCK_SNPS
    snp_block = jnp.arange(snps) // BLOCK_SNPS
    observed = (snp_block[None, :] != missing_codes[:, None]).astype(jnp.float32)
    dosage = genotypes.astype(jnp.float32) * observed
    moments = jnp.stack([jnp.sum(observed, 0), jnp.sum(dosage, 0), jnp.sum(dosage * dosage, 0)])
    masked = genotypes * observed.astype(jnp.bfloat16)
    crossed = jnp.einsum("rs,rb->sb", masked, probes, preferred_element_type=jnp.float32)
    one_hot = (missing_codes[:, None] == jnp.arange(2 * blocks)[None, :]).astype(jnp.bfloat16)
    per_code = jnp.einsum("rc,rb->cb", one_hot, probes, preferred_element_type=jnp.float32)
    moments, crossed, per_code = everywhere((moments, crossed, per_code))
    mean, inv_sd = statistics(moments)
    beside = jnp.sum(per_code, 0)[None, :] - jnp.repeat(per_code[:blocks], BLOCK_SNPS, axis=0)
    projection = inv_sd[:, None] * (crossed - mean[:, None] * beside) / math.sqrt(total_rows)
    standard = (
        (genotypes.astype(jnp.float32) - mean[None, :]) * inv_sd[None, :] * observed
    ).astype(jnp.bfloat16)
    projection = projection.astype(jnp.bfloat16)
    image = (
        jnp.dot(standard, projection, preferred_element_type=jnp.float32) / math.sqrt(snps)
    ).astype(jnp.bfloat16)
    gram = jnp.einsum("rb,rc->bc", image, image, preferred_element_type=jnp.float32)
    cross = jnp.einsum("rs,rb->sb", standard, image, preferred_element_type=jnp.float32)
    gram, cross = everywhere((gram, cross))
    lower = jnp.linalg.cholesky(gram)
    basis = jax.scipy.linalg.solve_triangular(
        lower, image.astype(jnp.float32).T, lower=True
    ).T * math.sqrt(total_rows)
    scores = jax.scipy.linalg.solve_triangular(lower, cross.T, lower=True).T * math.sqrt(
        snps / total_rows
    )
    return (basis.astype(jnp.bfloat16), scores.astype(jnp.bfloat16))


def solution(mesh):
    return jax.shard_map(
        per_device,
        mesh=mesh,
        in_specs=(P(("rows", "cols"), None), P(("rows", "cols"), None), P(("rows", "cols"))),
        out_specs=(P(("rows", "cols"), None), P()),
        check_vma=False,
    )
```

profile of v0, /device:TPU:0, one launch (start us, length us, event | category | flops | bytes accessed | tf_op | source)
XLA Modules:
  0.0 321.8 jit_solution(10941439607097090679)
XLA Ops:
  7.2 0.0 copy-start
  7.2 0.0 all-reduce.5.cloned.1.call-start
  7.2 0.9 copy-done
  8.1 0.0 copy-start.2
  8.1 4.8 %fusion.8 = f32[2048,128]{1,0:T(8,128)} fusion(bf16[960,128]{1,0:T(8,128)(2,1)S(1)} %copy-done, bf16[960,2048]{1,0:T(8,128)(2,1)} %param.3, s32[2048]{0:T(1024)S(1)} %add_select_fusion, s32[960]{0:T(1024)} %param.5), kind=kOutput, calls=%fused_computation.12 | convolution fusion | flops 511180800 | bytes 5238528 | tf_op jit(solution)/shard_map/rs,rb->sb/dot_general | solution.py:31
  12.9 0.0 all-reduce.5.cloned.1.call-update
  12.9 0.0 all-reduce.7.cloned.1.call-start
  13.0 0.0 copy-done.2
  13.0 0.4 fusion.20
  13.4 4.0 %fusion.3 = (f32[2048]{0:T(1024)S(1)}, f32[2048]{0:T(1024)S(1)}, f32[2048]{0:T(1024)S(1)}) fusion(bf16[960,2048]{1,0:T(8,128)(2,1)} %param.3, s32[2048]{0:T(1024)S(1)} %add_select_fusion, s32[960]{0:T(1024)S(1)} %copy-done.2), kind=kLoop, calls=%fused_computation.7 | loop fusion | flops 15722496 | bytes 3968768 | tf_op jit(solution)/shard_map/reduce_sum | solution.py:29
  17.5 42.6 %all-reduce = (f32[32,128]{1,0:T(8,128)S(1)}, f32[3,2048]{1,0:T(4,128)S(1)}) all-reduce(f32[32,128]{1,0:T(8,128)S(1)} %fusion.20, f32[3,2048]{1,0:T(4,128)S(1)} %pad_maximum_fusion), channel_id=1, replica_groups=mesh['rows'=4,'cols'=8] {'rows','cols'}, use_global_device_ids=true, to_apply=%region_5.6 | all-reduce | flops 10240 | bytes 81920 | tf_op jit(solution)/shard_map/psum | solution.py:12
  60.1 86.7 %all-reduce.5.cloned.1.call-done = f32[2048,128]{1,0:T(8,128)} async-done(((f32[2048,128]{1,0:T(8,128)}), f32[2048,128]{1,0:T(8,128)}) %all-reduce.5.cloned.1.call-update) | async-done | bytes 1048592 | tf_op jit(solution)/shard_map/psum | solution.py:12
  146.9 1.8 fusion.19
  148.6 0.0 copy-start.1
  148.6 3.6 %fusion.14 = bf16[960,128]{1,0:T(8,128)(2,1)S(1)} fusion(bf16[2048,128]{1,0:T(8,128)(2,1)S(1)} %fusion.19, bf16[960,2048]{1,0:T(8,128)(2,1)} %param.3, f32[2048]{0:T(1024)S(1)} %bitcast.45, f32[2048]{0:T(1024)S(1)} %bitcast.39, s32[2048]{0:T(1024)S(1)} %add_select_fusion, s32[960]{0:T(1024)S(1)} %copy-done.2), kind=kOutput, calls=%fused_computation.20 | convolution fusion | flops 515358720 | bytes 4730624 | tf_op jit(solution)/shard_map/dot_general | solution.py:43
  152.3 0.9 fusion.34
  153.2 0.0 copy-done.1
  153.2 2.9 fusion.22
  156.1 0.0 all-reduce.7.cloned.1.call-update
  156.2 130.1 %all-reduce.7.cloned.1.call-done = (f32[128,128]{0,1:T(8,128)}, f32[2048,128]{1,0:T(8,128)}) async-done(((f32[128,128]{0,1:T(8,128)}, f32[2048,128]{1,0:T(8,128)}), (f32[128,128]{0,1:T(8,128)}, f32[2048,128]{1,0:T(8,128)})) %all-reduce.7.cloned.1.call-update) | async-done | bytes 1114128 | tf_op jit(solution)/shard_map/psum | solution.py:12
  286.3 0.9 copy.6
  287.2 0.9 fusion.28
  288.1 11.7 %cholesky.16 = f32[128,128]{1,0:T(8,128)S(1)} custom-call(f32[128,128]{1,0:T(8,128)S(1)} %fusion.28), custom_call_target="Cholesky" | custom-call | tf_op jit(solution)/shard_map/jit(cholesky)/cholesky | solution.py:48
  299.8 0.6 compare_reduce_fusion
  300.5 0.7 fusion.25
  301.1 9.8 %custom-call.10 = f32[1,128,128]{1,2,0:T(8,128)S(1)} custom-call(f32[1,128,128]{2,1,0:T(8,128)S(1)} %fusion.25), custom_call_target="InvertDiagBlocksLowerTriangular" | custom-call | tf_op jit(solution)/shard_map/jit(_solve_triangular)/triangular_solve | solution.py:49
  310.9 1.1 fusion.13
  312.0 3.0 fusion.12
  (7 shorter events, 0.1 us)
Async XLA Ops:
  7.2 1.0 copy-start
  7.2 139.7 %all-reduce.5.cloned.1.call-start = ((), (), s32[]{:S(2)}) async-start(), calls=%async_computation | async-start | bytes 2097152 | tf_op jit(solution)/shard_map/psum | solution.py:12
  8.1 4.9 %copy-start.2 = (s32[960]{0:T(1024)S(1)}, s32[960]{0:T(1024)}, u32[]{:S(2)}) copy-start(s32[960]{0:T(1024)} %param.5) | copy-start | bytes 11524
  12.9 273.4 %all-reduce.7.cloned.1.call-start = ((), (), s32[]{:S(2)}) async-start(), calls=%async_computation.1 | async-start | bytes 2228224 | tf_op jit(solution)/shard_map/psum | solution.py:12
  148.6 4.6 %copy-start.1 = (bf16[960,2048]{1,0:T(8,128)(2,1)S(1)}, bf16[960,2048]{1,0:T(8,128)(2,1)}, u32[]{:S(2)}) copy-start(bf16[960,2048]{1,0:T(8,128)(2,1)} %param.3) | copy-start | bytes 11796484
Sparse Core Ops, SparseCore 0:
  13.2 133.6 all-reduce.4
  156.3 129.9 all-reduce.6
where the time goes:
time: 322 us
  waiting for transfers between devices  217 us (67%)
  blocking collectives  42.6 us (13%)
  other arithmetic  29.6 us (9%)
  matrix products  16.7 us (5%)
  between operations  14.2 us (4%)
    psum x2, waiting for transfers between devices, everywhere(): return lax.psum(values, ('rows', 'cols'))  217 us
    psum x1, blocking collectives, everywhere(): return lax.psum(values, ('rows', 'cols'))  42.6 us
    another operation x3, other arithmetic, per_device(): lower = jnp.linalg.cholesky(gram)  12.4 us
    another operation x2, other arithmetic, per_device(): jax.scipy.linalg.solve_triangular(lower, image.astype(jnp.float32).T, low...  10.5 us
  transfers between devices with their start and end apart: 2, of which 2 were waited for; matrix products, arithmetic and copies ran while one was open for 1% of the time, Pallas kernels for 0%

commit v1 on v0

v1 whole, which is shorter than its diff:
```python
import functools
import math

import jax
import jax.numpy as jnp
from jax import lax
from jax.experimental import pallas as pl
from jax.experimental.pallas import tpu as pltpu
from jax.sharding import PartitionSpec as P

MESH = pl.DeviceIdType.MESH
BLOCK_SNPS = 128
LANES = 128


def radices(n):
    bits = n.bit_length() - 1
    if n != 1 << bits:
        return [n]
    return [2] * (bits % 2) + [4] * (bits // 2)


def stage_list(sizes):
    stages = []
    for axis in ("cols", "rows"):
        stride = 1
        for radix in radices(sizes[axis]):
            stages.append((axis, stride, radix))
            stride *= radix
    return stages


class Plan:
    def __init__(self, rows, stages, scatter):
        self.rows, self.stages = rows, stages
        self.current, self.split = [rows], []
        for number, (_, _, radix) in enumerate(stages):
            now = self.current[-1]
            split = number in scatter and now % (8 * radix) == 0
            self.split.append(split)
            self.current.append(now // radix if split else now)
        self.copies = 2 * sum(radix - 1 for _, _, radix in stages)
        self.scratch = (
            [pltpu.VMEM((rows, LANES), jnp.float32)] * 2
            + [pltpu.VMEM((r, LANES), jnp.float32) for r in self.current[1:-1]]
            + [
                pltpu.VMEM((radix, r, LANES), jnp.float32)
                for (_, _, radix), r in zip(stages, self.current[1:])
            ]
            + [pltpu.SemaphoreType.DMA((self.copies,)), pltpu.SemaphoreType.DMA((self.copies,))]
        )


class Stream:
    def __init__(self, plan, refs):
        self.plan = plan
        n = len(plan.stages)
        self.source, self.full = refs[0], refs[1]
        self.parts = [refs[0], *refs[2 : n + 1]]
        self.landing = refs[n + 1 : 2 * n + 1]
        self.send_sem, self.recv_sem = refs[2 * n + 1], refs[2 * n + 2]
        self.pending, self.flight, self.used = [], {}, 0
        self.offsets = [0]
        for number, (axis, stride, radix) in enumerate(plan.stages):
            offset = self.offsets[-1]
            if plan.split[number]:
                offset = offset + self.digit(number) * plan.current[number + 1]
            self.offsets.append(offset)

    def digit(self, number):
        axis, stride, radix = self.plan.stages[number]
        return lax.rem(lax.axis_index(axis) // stride, radix)

    def peer(self, number, step):
        axis, stride, radix = self.plan.stages[number]
        digit = self.digit(number)
        other = lax.rem(digit + step, radix)
        return other, {axis: lax.axis_index(axis) + (other - digit) * stride}

    def start(self, key, source, target, device):
        copy = pltpu.make_async_remote_copy(
            src_ref=source,
            dst_ref=target,
            send_sem=self.send_sem.at[self.used],
            recv_sem=self.recv_sem.at[self.used],
            device_id=device,
            device_id_type=MESH,
        )
        self.used += 1
        copy.start()
        self.pending.append(copy)
        self.flight.setdefault(key, []).append(copy)

    def arrive(self, key):
        for copy in self.flight.pop(key):
            copy.wait_recv()

    def send(self, number):
        rows = self.plan.current[number + 1]
        here = self.parts[number]
        for step in range(1, self.plan.stages[number][2]):
            other, device = self.peer(number, step)
            if self.plan.split[number]:
                source = here.at[pl.ds(pl.multiple_of(other * rows, 8), rows)]
            else:
                source = here
            self.start(("out", number), source, self.landing[number].at[self.digit(number)], device)

    def receive(self, number):
        plan = self.plan
        rows, radix = plan.current[number + 1], plan.stages[number][2]
        here, landing, digit = self.parts[number], self.landing[number], self.digit(number)
        if plan.split[number]:
            own = here[pl.ds(pl.multiple_of(digit * rows, 8), rows)]
        else:
            own = here[...]
        landing[digit] = own
        self.arrive(("out", number))
        total = landing[0]
        for other in range(1, radix):
            total = total + landing[other]
        if number + 1 < len(plan.stages):
            self.parts[number + 1][...] = total
        else:
            self.full[pl.ds(pl.multiple_of(self.offsets[-1], 8), rows)] = total

    def spread(self, number):
        if not self.plan.split[number]:
            return
        rows = self.plan.current[number + 1]
        block = self.full.at[pl.ds(pl.multiple_of(self.offsets[number + 1], 8), rows)]
        for step in range(1, self.plan.stages[number][2]):
            _, device = self.peer(number, step)
            self.start(("back", number), block, block, device)

    def gather(self, number):
        if self.plan.split[number]:
            self.arrive(("back", number))

    def finish(self):
        for copy in self.pending:
            copy.wait_send()


def factor(state, columns):
    size = BLOCK_SNPS
    row_at = lax.broadcasted_iota(jnp.int32, (size, size), 0)
    lane_at = lax.broadcasted_iota(jnp.int32, (size, size), 1)

    def step(j, pair):
        left, right = pair
        here = row_at == j
        row = jnp.sum(jnp.where(here, left, 0.0), axis=0, keepdims=True)
        column = jnp.sum(jnp.where(lane_at == j, left, 0.0), axis=1, keepdims=True)
        right_row = jnp.sum(jnp.where(here, right, 0.0), axis=0, keepdims=True)
        pivot = jnp.sum(jnp.where(lane_at[:1] == j, row, 0.0), axis=1, keepdims=True)
        scale = 1.0 / jnp.sqrt(pivot)
        column = jnp.where(row_at > j, column * scale, 0.0)
        left = left - column * (row * scale)
        right_row = right_row * scale
        right = jnp.where(here, right_row, right - column * right_row)
        return left, right

    return lax.fori_loop(*columns, step, state)


def body(sizes, plans, n_inputs, *refs):
    geno_hbm, probes_ref, codes_ref, basis_ref, scores_ref = refs[:5]
    geno, projection, load_sem = refs[5:8]
    rest = refs[8:]
    streams = []
    for plan in plans:
        streams.append(Stream(plan, rest[: len(plan.scratch)]))
        rest = rest[len(plan.scratch) :]
    first, small, second, square_sums = streams
    rows, snps = geno.shape
    blocks = snps // BLOCK_SNPS
    total_rows = rows * sizes["rows"] * sizes["cols"]
    stages = plans[0].stages
    count = len(stages)

    loads = []
    for b in range(blocks):
        cut = pl.ds(b * BLOCK_SNPS, BLOCK_SNPS)
        load = pltpu.make_async_copy(geno_hbm.at[:, cut], geno.at[:, cut], load_sem.at[b])
        load.start()
        loads.append(load)

    barrier = pltpu.get_barrier_semaphore()
    peers = 0
    for number, (_, _, radix) in enumerate(stages):
        for step in range(1, radix):
            _, device = first.peer(number, step)
            pl.semaphore_signal(barrier, inc=1, device_id=device, device_id_type=MESH)
            peers += 1

    probes = probes_ref[...]
    probes_t = probes.astype(jnp.float32).T.astype(jnp.bfloat16)
    codes = codes_ref[...]
    lane = lax.broadcasted_iota(jnp.int32, (rows, LANES), 1)
    seen = (codes != lane).astype(jnp.float32).astype(jnp.bfloat16)
    contract = (((0,), (0,)), ((), ()))
    small.source[0:blocks] = lax.dot_general(
        seen, probes, contract, preferred_element_type=jnp.float32
    )[:blocks]
    small.source[3 * blocks : 4 * blocks] = lax.dot_general(
        seen, jnp.ones_like(probes), contract, preferred_element_type=jnp.float32
    )[:blocks]
    for b in range(blocks):
        cut = slice(b * BLOCK_SNPS, (b + 1) * BLOCK_SNPS)
        loads[b].wait()
        dosage = jnp.where(codes != b, geno[:, cut].astype(jnp.float32), 0.0)
        small.source[blocks + b : blocks + b + 1] = jnp.sum(dosage, axis=0, keepdims=True)
        small.source[2 * blocks + b : 2 * blocks + b + 1] = jnp.sum(
            dosage * dosage, axis=0, keepdims=True
        )
        first.source[cut] = jnp.dot(
            probes_t, dosage.astype(jnp.bfloat16), preferred_element_type=jnp.float32
        )
    pl.semaphore_wait(barrier, peers)

    for number in range(count):
        small.send(number)
        first.send(number)
        small.receive(number)
        first.receive(number)
    for number in reversed(range(count)):
        small.spread(number)
    first.spread(count - 1)
    for number in reversed(range(count)):
        small.gather(number)
    moments = small.full
    counted = jnp.maximum(moments[3 * blocks : 4 * blocks], 1.0)
    mean = moments[blocks : 2 * blocks] / counted
    inv_sd = 1.0 / jnp.sqrt(moments[2 * blocks : 3 * blocks] / counted - mean * mean + 1e-05)
    beside = moments[0:blocks].T
    for number in reversed(range(count)):
        first.gather(number)
        if number:
            first.spread(number - 1)
        if number == count - 1:
            for b in range(blocks):
                cut = slice(b * BLOCK_SNPS, (b + 1) * BLOCK_SNPS)
                centred = (geno[:, cut].astype(jnp.float32) - mean[b : b + 1]) * inv_sd[b : b + 1]
                geno[:, cut] = jnp.where(codes != b, centred, 0.0).astype(jnp.bfloat16)
    for b in range(blocks):
        cut = slice(b * BLOCK_SNPS, (b + 1) * BLOCK_SNPS)
        value = inv_sd[b : b + 1] * (first.full[cut] - mean[b : b + 1] * beside[:, b : b + 1])
        projection[:, cut] = (value / math.sqrt(total_rows)).astype(jnp.bfloat16)

    image = lax.dot_general(
        geno[...], projection[...], (((1,), (1,)), ((), ())), preferred_element_type=jnp.float32
    )
    image = (image / math.sqrt(snps)).astype(jnp.bfloat16)
    image_t = image.astype(jnp.float32).T.astype(jnp.bfloat16)
    square_sums.source[...] = jnp.dot(image_t, image, preferred_element_type=jnp.float32)
    square_sums.send(0)
    for b in range(blocks):
        cut = slice(b * BLOCK_SNPS, (b + 1) * BLOCK_SNPS)
        second.source[cut] = jnp.dot(image_t, geno[:, cut], preferred_element_type=jnp.float32)
    for number in range(count):
        if number:
            square_sums.send(number)
        second.send(number)
        square_sums.receive(number)
        second.receive(number)
    second.spread(count - 1)
    for number in reversed(range(count)):
        square_sums.spread(number)
        square_sums.gather(number)
    eye = (
        lax.broadcasted_iota(jnp.int32, (LANES, LANES), 0)
        == lax.broadcasted_iota(jnp.int32, (LANES, LANES), 1)
    ).astype(jnp.float32)
    state = (square_sums.full[...], eye)
    for number in reversed(range(count)):
        done = count - 1 - number
        state = factor(state, (LANES * done // count, LANES * (done + 1) // count))
        second.gather(number)
        if number:
            second.spread(number - 1)
    inverse = state[1]
    basis = lax.dot_general(
        image.astype(jnp.float32),
        inverse,
        (((1,), (1,)), ((), ())),
        preferred_element_type=jnp.float32,
        precision=lax.Precision.HIGHEST,
    )
    basis_ref[...] = (basis * math.sqrt(total_rows)).astype(jnp.bfloat16)
    for b in range(blocks):
        cut = slice(b * BLOCK_SNPS, (b + 1) * BLOCK_SNPS)
        score = jnp.dot(
            inverse,
            second.full[cut],
            preferred_element_type=jnp.float32,
            precision=lax.Precision.HIGHEST,
        )
        scores_ref[cut] = (score.T * math.sqrt(snps / total_rows)).astype(jnp.bfloat16)
    for stream in streams:
        stream.finish()


def per_device(sizes, genotypes, probes, missing_codes):
    rows, snps = genotypes.shape
    stages = stage_list(sizes)
    everything = range(len(stages))
    plans = [
        Plan(snps, stages, everything),
        Plan(4 * snps // BLOCK_SNPS, stages, (0,)),
        Plan(snps, stages, everything),
        Plan(probes.shape[1], stages, (0,)),
    ]
    scratch = [
        pltpu.VMEM((rows, snps), jnp.bfloat16),
        pltpu.VMEM((LANES, snps), jnp.bfloat16),
        pltpu.SemaphoreType.DMA((snps // BLOCK_SNPS,)),
    ]
    for plan in plans:
        scratch += plan.scratch
    vmem = pl.BlockSpec(memory_space=pltpu.VMEM)
    return pl.pallas_call(
        functools.partial(body, sizes, plans, 3),
        out_shape=(
            jax.ShapeDtypeStruct((rows, LANES), jnp.bfloat16),
            jax.ShapeDtypeStruct((snps, LANES), jnp.bfloat16),
        ),
        in_specs=[pl.BlockSpec(memory_space=pl.ANY), vmem, vmem],
        out_specs=(vmem, vmem),
        scratch_shapes=scratch,
        compiler_params=pltpu.CompilerParams(
            collective_id=0, has_side_effects=True, vmem_limit_bytes=48 * 1024 * 1024
        ),
    )(genotypes, probes, missing_codes[:, None])


def solution(mesh):
    return jax.shard_map(
        functools.partial(per_device, dict(mesh.shape)),
        mesh=mesh,
        in_specs=(P(("rows", "cols"), None), P(("rows", "cols"), None), P(("rows", "cols"))),
        out_specs=(P(("rows", "cols"), None), P()),
        check_vma=False,
    )
```

time: 322 us -> 90.2 us (0.28)
  waiting for transfers between devices: 217 us -> 0 us
  Pallas kernels: 0 us -> 83.9 us
  blocking collectives: 42.6 us -> 0 us
  other arithmetic: 29.6 us -> 0 us
  matrix products: 16.7 us -> 0 us
  between operations: 14.2 us -> 0.65 us
  local copies, waits for them, and re-layouts: 1.82 us -> 5.44 us
    psum x2 -> x0, waiting for transfers between devices: 217 us -> none  [everywhere(): return lax.psum(values, ('rows', 'cols'))]
    pallas_call x0 -> x1, Pallas kernels: none -> 83.9 us  [per_device(): pl.pallas_call(functools.partial(body, sizes, plans, 3), out_shape=(jax.S...]
    psum x1 -> x0, blocking collectives: 42.6 us -> none  [everywhere(): return lax.psum(values, ('rows', 'cols'))]
    another operation x6 -> x0, other arithmetic: 22.9 us -> none  [the longest x3 12.4 us: per_device(): lower = jnp.linalg.cholesky(gram)]
    dot_general x5 -> x0, matrix products: 12.7 us -> none  [the longest x1 4.78 us: per_device(): jnp.einsum('rs,rb->sb', masked, probes, preferred_element_type=jnp.float32)]
    another operation x2 -> x0, matrix products: 4.04 us -> none  [the longest x1 2.99 us: per_device(): jax.scipy.linalg.solve_triangular(lower, cross.T, lower=True)]
    reduce_sum x2 -> x0, other arithmetic: 4.03 us -> none  [the longest x1 4.01 us: per_device(): jnp.sum(dosage, 0)]
    unnamed x6, local copies, waits for them, and re-layouts: 0.9 us -> 4.54 us
  transfers between devices with their start and end apart: 2 -> 0, of which waited for: 2 -> 0; matrix products, arithmetic and copies ran while one was open for 1% -> 0% of each run, Pallas kernels for 0% -> 0%
where the time goes in v1:
time: 90.2 us; the launch traced here: 90 us
  Pallas kernels  83.9 us (93%)
  local copies, waits for them, and re-layouts  5.44 us (6%)
    pallas_call x1, Pallas kernels, per_device(): pl.pallas_call(functools.partial(body, sizes, plans, 3), out_shape=(jax.S...  83.9 us
    unnamed x6, local copies, waits for them, and re-layouts  4.54 us

profile of v1, /device:TPU:0, one launch (start us, length us, event | category | flops | bytes accessed | tf_op | source)
XLA Modules:
  0.0 90.0 jit_solution(13579477077963411059)
XLA Ops:
  0.6 0.9 copy.5.refs_2_
  1.5 0.0 copy-start
  1.5 2.1 %copy-done = bf16[960,2048]{1,0:T(8,128)(2,1)S(1)} copy-done((bf16[960,2048]{1,0:T(8,128)(2,1)S(1)}, bf16[960,2048]{1,0:T(8,128)(2,1)}, u32[]{:S(2)}) %copy-start) | copy-done | bytes 3932184
  3.6 0.0 copy-start.1
  3.7 0.9 %copy-done.1 = bf16[960,128]{1,0:T(8,128)(2,1)S(1)} copy-done((bf16[960,128]{1,0:T(8,128)(2,1)S(1)}, bf16[960,128]{1,0:T(8,128)(2,1)}, u32[]{:S(2)}) %copy-start.1) | copy-done | bytes 245784
  4.6 83.9 %shard_map.50 = (bf16[960,128]{1,0:T(8,128)(2,1)S(1)}, bf16[2048,128]{1,0:T(8,128)(2,1)S(1)}) custom-call(bf16[960,2048]{1,0:T(8,128)(2,1)S(1)} %copy-done, bf16[960,128]{1,0:T(8,128)(2,1)S(1)} %copy-done.1, s32[960,1]{1,0:T(8,128)S(1)} %copy.5.refs_2_), custom_call_target="tpu_custom_call" | custom-call | tf_op jit(solution)/shard_map/pallas_call | solution.py:322
  88.5 0.7 copy.8
  89.2 0.8 copy.9
Async XLA Ops:
  1.5 2.1 %copy-start = (bf16[960,2048]{1,0:T(8,128)(2,1)S(1)}, bf16[960,2048]{1,0:T(8,128)(2,1)}, u32[]{:S(2)}) copy-start(bf16[960,2048]{1,0:T(8,128)(2,1)} %refs_0_.1) | copy-start | bytes 11796484
  3.6 0.9 %copy-start.1 = (bf16[960,128]{1,0:T(8,128)(2,1)S(1)}, bf16[960,128]{1,0:T(8,128)(2,1)}, u32[]{:S(2)}) copy-start(bf16[960,128]{1,0:T(8,128)(2,1)} %refs_1_.1) | copy-start | bytes 737284

commit v2 on v1

--- a/solution.py
+++ b/solution.py
@@ -164,6 +164,19 @@
     return lax.fori_loop(*columns, step, state)
 
 
+def exchange(count, little, pair):
+    for number in range(count):
+        little.receive(number)
+        if number + 1 < count:
+            little.send(number + 1)
+        for stream in pair:
+            stream.receive(number)
+            if number + 1 < count:
+                stream.send(number + 1)
+            else:
+                stream.spread(number)
+
+
 def body(sizes, plans, n_inputs, *refs):
     geno_hbm, probes_ref, codes_ref, basis_ref, scores_ref = refs[:5]
     geno, projection, load_sem = refs[5:8]
@@ -172,9 +185,15 @@
     for plan in plans:
         streams.append(Stream(plan, rest[: len(plan.scratch)]))
         rest = rest[len(plan.scratch) :]
-    first, small, second, square_sums = streams
+    firsts, seconds, (small, square_sums) = streams[0:2], streams[2:4], streams[4:6]
     rows, snps = geno.shape
     blocks = snps // BLOCK_SNPS
+    half = blocks // 2
+
+    def place(b):
+        start = b % half * BLOCK_SNPS
+        return b // half, slice(start, start + BLOCK_SNPS)
+
     total_rows = rows * sizes["rows"] * sizes["cols"]
     stages = plans[0].stages
     count = len(stages)
@@ -190,7 +209,7 @@
     peers = 0
     for number, (_, _, radix) in enumerate(stages):
         for step in range(1, radix):
-            _, device = first.peer(number, step)
+            _, device = firsts[0].peer(number, step)
             pl.semaphore_signal(barrier, inc=1, device_id=device, device_id_type=MESH)
             peers += 1
 
@@ -214,19 +233,18 @@
         small.source[2 * blocks + b : 2 * blocks + b + 1] = jnp.sum(
             dosage * dosage, axis=0, keepdims=True
         )
-        first.source[cut] = jnp.dot(
+        which, spot = place(b)
+        firsts[which].source[spot] = jnp.dot(
             probes_t, dosage.astype(jnp.bfloat16), preferred_element_type=jnp.float32
         )
-    pl.semaphore_wait(barrier, peers)
-
-    for number in range(count):
-        small.send(number)
-        first.send(number)
-        small.receive(number)
-        first.receive(number)
+        if b == half - 1:
+            pl.semaphore_wait(barrier, peers)
+            firsts[0].send(0)
+    small.send(0)
+    firsts[1].send(0)
+    exchange(count, small, firsts)
     for number in reversed(range(count)):
         small.spread(number)
-    first.spread(count - 1)
     for number in reversed(range(count)):
         small.gather(number)
     moments = small.full
@@ -235,17 +253,19 @@
     inv_sd = 1.0 / jnp.sqrt(moments[2 * blocks : 3 * blocks] / counted - mean * mean + 1e-05)
     beside = moments[0:blocks].T
     for number in reversed(range(count)):
-        first.gather(number)
-        if number:
-            first.spread(number - 1)
-        if number == count - 1:
-            for b in range(blocks):
-                cut = slice(b * BLOCK_SNPS, (b + 1) * BLOCK_SNPS)
-                centred = (geno[:, cut].astype(jnp.float32) - mean[b : b + 1]) * inv_sd[b : b + 1]
-                geno[:, cut] = jnp.where(codes != b, centred, 0.0).astype(jnp.bfloat16)
+        turn = count - 1 - number
+        for b in range(half * turn, half * (turn + 1) if turn < 2 else half * turn):
+            cut = slice(b * BLOCK_SNPS, (b + 1) * BLOCK_SNPS)
+            centred = (geno[:, cut].astype(jnp.float32) - mean[b : b + 1]) * inv_sd[b : b + 1]
+            geno[:, cut] = jnp.where(codes != b, centred, 0.0).astype(jnp.bfloat16)
+        for stream in firsts:
+            stream.gather(number)
+            if number:
+                stream.spread(number - 1)
     for b in range(blocks):
         cut = slice(b * BLOCK_SNPS, (b + 1) * BLOCK_SNPS)
-        value = inv_sd[b : b + 1] * (first.full[cut] - mean[b : b + 1] * beside[:, b : b + 1])
+        which, spot = place(b)
+        value = inv_sd[b : b + 1] * (firsts[which].full[spot] - mean[b : b + 1] * beside[:, b : b + 1])
         projection[:, cut] = (value / math.sqrt(total_rows)).astype(jnp.bfloat16)
 
     image = lax.dot_general(
@@ -257,14 +277,13 @@
     square_sums.send(0)
     for b in range(blocks):
         cut = slice(b * BLOCK_SNPS, (b + 1) * BLOCK_SNPS)
-        second.source[cut] = jnp.dot(image_t, geno[:, cut], preferred_element_type=jnp.float32)
-    for number in range(count):
-        if number:
-            square_sums.send(number)
-        second.send(number)
-        square_sums.receive(number)
-        second.receive(number)
-    second.spread(count - 1)
+        which, spot = place(b)
+        seconds[which].source[spot] = jnp.dot(
+            image_t, geno[:, cut], preferred_element_type=jnp.float32
+        )
+        if b % half == half - 1:
+            seconds[which].send(0)
+    exchange(count, square_sums, seconds)
     for number in reversed(range(count)):
         square_sums.spread(number)
         square_sums.gather(number)
@@ -276,9 +295,10 @@
     for number in reversed(range(count)):
         done = count - 1 - number
         state = factor(state, (LANES * done // count, LANES * (done + 1) // count))
-        second.gather(number)
-        if number:
-            second.spread(number - 1)
+        for stream in seconds:
+            stream.gather(number)
+            if number:
+                stream.spread(number - 1)
     inverse = state[1]
     basis = lax.dot_general(
         image.astype(jnp.float32),
@@ -292,7 +312,7 @@
         cut = slice(b * BLOCK_SNPS, (b + 1) * BLOCK_SNPS)
         score = jnp.dot(
             inverse,
-            second.full[cut],
+            seconds[place(b)[0]].full[place(b)[1]],
             preferred_element_type=jnp.float32,
             precision=lax.Precision.HIGHEST,
         )
@@ -305,10 +325,13 @@
     rows, snps = genotypes.shape
     stages = stage_list(sizes)
     everything = range(len(stages))
+    turned = stages[:1] + stages[:0:-1]
     plans = [
-        Plan(snps, stages, everything),
+        Plan(snps // 2, stages, everything),
+        Plan(snps // 2, turned, everything),
+        Plan(snps // 2, stages, everything),
+        Plan(snps // 2, turned, everything),
         Plan(4 * snps // BLOCK_SNPS, stages, (0,)),
-        Plan(snps, stages, everything),
         Plan(probes.shape[1], stages, (0,)),
     ]
     scratch = [

time: 90.2 us -> 82.5 us (0.915)
  Pallas kernels: 83.9 us -> 75.5 us
    pallas_call x1, Pallas kernels: 83.9 us -> 75.5 us  [per_device(): pl.pallas_call(functools.partial(body, sizes, plans, 3), out_shape=(jax.S...]
where the time goes in v2:
time: 82.5 us; the launch traced here: 81.5 us
  Pallas kernels  75.5 us (92%)
  local copies, waits for them, and re-layouts  5.44 us (7%)
    pallas_call x1, Pallas kernels, per_device(): pl.pallas_call(functools.partial(body, sizes, plans, 3), out_shape=(jax.S...  75.5 us
    unnamed x6, local copies, waits for them, and re-layouts  4.54 us

profile of v2, /device:TPU:0, one launch (start us, length us, event | category | flops | bytes accessed | tf_op | source)
XLA Modules:
  0.0 81.5 jit_solution(15055749362587835920)
XLA Ops:
  0.6 0.9 %copy.5.refs_2_ = s32[960,1]{1,0:T(8,128)S(1)} copy(s32[960,1]{0,1:T(1,128)} %bitcast.1) | data formatting | bytes 7680 | tf_op jit(solution)/shard_map/broadcast_in_dim | solution.py:357
  1.5 0.0 copy-start
  1.5 2.1 %copy-done = bf16[960,2048]{1,0:T(8,128)(2,1)S(1)} copy-done((bf16[960,2048]{1,0:T(8,128)(2,1)S(1)}, bf16[960,2048]{1,0:T(8,128)(2,1)}, u32[]{:S(2)}) %copy-start) | copy-done | bytes 3932184
  3.6 0.0 copy-start.1
  3.7 0.9 %copy-done.1 = bf16[960,128]{1,0:T(8,128)(2,1)S(1)} copy-done((bf16[960,128]{1,0:T(8,128)(2,1)S(1)}, bf16[960,128]{1,0:T(8,128)(2,1)}, u32[]{:S(2)}) %copy-start.1) | copy-done | bytes 245784
  4.6 75.5 %shard_map.50 = (bf16[960,128]{1,0:T(8,128)(2,1)S(1)}, bf16[2048,128]{1,0:T(8,128)(2,1)S(1)}) custom-call(bf16[960,2048]{1,0:T(8,128)(2,1)S(1)} %copy-done, bf16[960,128]{1,0:T(8,128)(2,1)S(1)} %copy-done.1, s32[960,1]{1,0:T(8,128)S(1)} %copy.5.refs_2_), custom_call_target="tpu_custom_call" | custom-call | tf_op jit(solution)/shard_map/pallas_call | solution.py:345
  80.1 0.7 copy.8
  80.8 0.8 copy.9
Async XLA Ops:
  1.5 2.1 %copy-start = (bf16[960,2048]{1,0:T(8,128)(2,1)S(1)}, bf16[960,2048]{1,0:T(8,128)(2,1)}, u32[]{:S(2)}) copy-start(bf16[960,2048]{1,0:T(8,128)(2,1)} %refs_0_.1) | copy-start | bytes 11796484
  3.6 0.9 %copy-start.1 = (bf16[960,128]{1,0:T(8,128)(2,1)S(1)}, bf16[960,128]{1,0:T(8,128)(2,1)}, u32[]{:S(2)}) copy-start(bf16[960,128]{1,0:T(8,128)(2,1)} %refs_1_.1) | copy-start | bytes 737284
